TPU v7x, 32 devices: a whole 2x2x4 slice. The times are simulated.
32 devices in a mesh: seq: 4 (over y, x), tp: 8 (over z, core).
Axes of the slice: x: 2, y: 2, z: 4, core: 2. Of those that a mesh axis runs over, the one named last changes fastest.
Arguments:
- hidden: bfloat16 [4096, 4096], P(('seq', 'tp')), may hold values from -6 to 6
- norm_gain: float32 [4096], replicated, may hold values from 0.5 to 1.5
- inner_weight: bfloat16 [4096, 2, 2048], P(None, None, 'tp'), may hold values from -0.09375 to 0.09375
- group_weight: bfloat16 [4096, 1024], P(None, 'tp'), may hold values from -0.09375 to 0.09375
- step_weight: bfloat16 [4096, 32], P(None, 'tp'), may hold values from -0.09375 to 0.09375
- step_bias: float32 [32], P('tp'), may hold values from -2 to 1
- decay_rate: float32 [32], P('tp'), may hold values from 0.0001 to 0.1
- filter_inner: bfloat16 [4, 2048], P(None, 'tp'), may hold values from -3 to 3
- filter_group: bfloat16 [4, 1024], P(None, 'tp'), may hold values from -3 to 3
- skip_gain: float32 [32], P('tp'), may hold values from 0.5 to 1.5
- mixer_gain: float32 [2048], P('tp'), may hold values from 0.5 to 1.5
- output_weight: bfloat16 [2048, 4096], P('tp'), may hold values from -0.125 to 0.125
- segment_ids: int32 [4096], replicated, may hold values from 0 to 3, never falling along the last dimension, each value on 1 to 2048 neighbouring positions
Outputs:
- layer_out: bfloat16 [4096, 4096], P(('seq', 'tp'))
Inputs may be any that keep to these rules, and one draw needn't show every extreme that they name: `segment_ids`: ids never fall along the pack; every id names at least one token, and one request has exactly 2048 tokens.
All inputs are finite; a program needn't handle non-finite values.
Results may differ from a plain program's by a relative error of at most 0.0051.
Values may be sent and summed in bfloat16 or wider, within the bound.
A program may use at most 128 MiB of HBM per device.

v0:
```python
import jax
import jax.numpy as jnp
from jax import lax
from jax.sharding import PartitionSpec as P

STRETCH = 256
EPS = 1e-05
HIGH = lax.Precision.HIGHEST


def swapped(block, axis, stride):
    count = lax.axis_size(axis)
    route = []
    for low in range(count):
        high = low | 1 << stride
        if high != low and high < count:
            route += [(low, high), (high, low)]
    return lax.ppermute(block, axis, route)


def from_behind(array, axis, by):
    size = lax.axis_size(axis)
    pairs = [(i, i + by) for i in range(size) if 0 <= i + by < size]
    return lax.ppermute(array, axis, pairs)


def entering_2(value, axis, join, neutral):
    count, mine = (lax.axis_size(axis), lax.axis_index(axis))
    pieces = jax.tree.map(lambda part: lax.all_gather(part, axis), value)
    total = jax.tree.map(
        lambda part, zero: jnp.full_like(part, 0) + jnp.asarray(zero, part.dtype), value, neutral
    )

    def hop(position, total):
        longer = join(total, jax.tree.map(lambda part: part[position], pieces))
        return jax.tree.map(lambda new, old: jnp.where(position < mine, new, old), longer, total)

    return lax.fori_loop(0, count - 1, hop, total)


def combine(earlier, later):
    return (earlier[0] * later[0], later[0][:, None, None] * earlier[1] + later[1])


def body(
    hidden,
    norm_gain,
    inner_weight,
    group_weight,
    step_weight,
    step_bias,
    decay_rate,
    filter_inner,
    filter_group,
    skip_gain,
    mixer_gain,
    output_weight,
    segment_ids,
):
    rows = hidden.shape[0]
    length = rows * lax.axis_size("tp")
    width = hidden.shape[1]
    inner_dev = inner_weight.shape[2]
    heads_dev = step_weight.shape[1]
    head_dim = inner_dev // heads_dev
    state_dim = group_weight.shape[1]
    taps = filter_inner.shape[0]
    first_row = lax.axis_index("seq") * length
    is_first = lax.axis_index("tp") % 2 == 0
    hidden_f = hidden.astype(jnp.float32)
    normed = (
        hidden_f
        * lax.rsqrt(jnp.mean(hidden_f * hidden_f, axis=-1, keepdims=True) + EPS)
        * norm_gain
    ).astype(jnp.bfloat16)
    other_weight, other_filter = swapped((group_weight, filter_group), "tp", 0)
    group_cols = (
        jnp.where(is_first, group_weight, other_weight),
        jnp.where(is_first, other_weight, group_weight),
    )
    filters = jnp.concatenate(
        [
            filter_inner,
            jnp.where(is_first, filter_group, other_filter),
            jnp.where(is_first, other_filter, filter_group),
        ],
        axis=1,
    )
    matrices = (inner_weight.reshape(width, 2 * inner_dev),) + group_cols + (step_weight,)
    piece = lax.all_gather(normed, "tp", axis=0, tiled=True)
    projected = jnp.concatenate(
        [jnp.dot(piece, matrix, preferred_element_type=jnp.float32) for matrix in matrices], axis=1
    )
    gate_z = projected[:, :inner_dev]
    conv_in = projected[:, inner_dev:-heads_dev]
    step_raw = projected[:, -heads_dev:]
    seg_pad = jnp.concatenate([jnp.full((taps - 1,), -1, jnp.int32), segment_ids])
    seg_ext = lax.dynamic_slice_in_dim(seg_pad, first_row, length + taps - 1)
    seg_local = seg_ext[taps - 1 :]
    before = from_behind(conv_in[length - (taps - 1) :], "seq", 1)
    extended = jnp.concatenate([before, conv_in], axis=0)
    filters_f = filters.astype(jnp.float32)
    total = jnp.zeros_like(conv_in)
    for offset in range(taps):
        same = (seg_ext[offset : offset + length] == seg_local).astype(jnp.float32)
        total = total + filters_f[offset] * extended[offset : offset + length] * same[:, None]
    active = jax.nn.silu(total)
    inner_x = active[:, :inner_dev]
    input_map = active[:, inner_dev : inner_dev + state_dim]
    output_map = active[:, inner_dev + state_dim :]
    starts = seg_local != seg_ext[taps - 2 : taps - 2 + length]
    step = jax.nn.softplus(step_raw + step_bias)
    log_decay = -step * decay_rate
    blocks = length // STRETCH
    block_x = inner_x.reshape(blocks, STRETCH, heads_dev, head_dim)
    block_b = input_map.reshape(blocks, STRETCH, state_dim)
    block_c = output_map.reshape(blocks, STRETCH, state_dim)
    step_heads = step.reshape(blocks, STRETCH, heads_dev).transpose(0, 2, 1)
    cumul = jnp.cumsum(log_decay.reshape(blocks, STRETCH, heads_dev), axis=1).transpose(0, 2, 1)
    block_seg = seg_local.reshape(blocks, STRETCH)
    block_start = starts.reshape(blocks, STRETCH)
    causal = jnp.tril(jnp.ones((STRETCH, STRETCH), jnp.bool_))
    same_seg = ((block_seg[:, :, None] == block_seg[:, None, :]) & causal)[:, None]
    gaps = cumul[:, :, :, None] - cumul[:, :, None, :]
    decay = jnp.where(same_seg, jnp.exp(jnp.where(same_seg, gaps, 0.0)), 0.0)
    products = jnp.einsum("cin,cjn->cij", block_c, block_b, precision=HIGH)
    mixing = decay * products[:, None] * step_heads[:, :, None, :]
    local_y = jnp.einsum("chij,cjhp->cihp", mixing, block_x, precision=HIGH)
    same_last = (block_seg == block_seg[:, -1:])[:, None, :]
    last_gap = cumul[:, :, -1:] - cumul
    end_weight = (
        jnp.where(same_last, jnp.exp(jnp.where(same_last, last_gap, 0.0)), 0.0) * step_heads
    )
    block_state = jnp.einsum("chj,cjhp,cjn->chpn", end_weight, block_x, block_b, precision=HIGH)
    clean = jnp.logical_not(jnp.any(block_start, axis=1)).astype(jnp.float32)
    block_keep = jnp.exp(cumul[:, :, -1]) * clean[:, None]

    def carry_blocks(carry, inputs):
        acc_state, acc_keep = carry
        keep, fresh = inputs
        return ((keep[:, None, None] * acc_state + fresh, acc_keep * keep), (acc_state, acc_keep))

    empty_state = jnp.zeros((heads_dev, head_dim, state_dim), jnp.float32)
    unit_keep = jnp.ones((heads_dev,), jnp.float32)
    (device_state, device_keep), (prior_state, prior_keep) = lax.scan(
        carry_blocks, (empty_state, unit_keep), (block_keep, block_state)
    )
    entering = entering_2((device_keep, device_state), "seq", combine, (unit_keep, empty_state))
    incoming = entering[1]
    entry_state = prior_state + prior_keep[:, :, None, None] * incoming[None]
    alive = (jnp.cumsum(block_start.astype(jnp.int32), axis=1) == 0).astype(jnp.float32)
    entry_weight = jnp.exp(cumul) * alive[:, None, :]
    carried_y = jnp.einsum("chi,cin,chpn->cihp", entry_weight, block_c, entry_state, precision=HIGH)
    ssm_out = (local_y + carried_y).reshape(length, heads_dev, head_dim) + skip_gain[
        None, :, None
    ] * inner_x.reshape(length, heads_dev, head_dim)
    gated = ssm_out.reshape(length, inner_dev) * jax.nn.silu(gate_z)
    own_squares = jnp.sum(gated * gated, axis=-1)
    other_squares = swapped(own_squares, "tp", 0)
    group_mean = (own_squares + other_squares) / (2 * inner_dev)
    mixed = (gated * lax.rsqrt(group_mean + EPS)[:, None] * mixer_gain).astype(jnp.bfloat16)
    partial_out = jnp.dot(mixed, output_weight, preferred_element_type=jnp.float32)
    mine = lax.psum_scatter(partial_out, "tp", scatter_dimension=0, tiled=True)
    return (hidden_f + mine).astype(jnp.bfloat16)


def solution(mesh):
    in_specs = (
        P(("seq", "tp"), None),
        P(),
        P(None, None, "tp"),
        P(None, "tp"),
        P(None, "tp"),
        P("tp"),
        P("tp"),
        P(None, "tp"),
        P(None, "tp"),
        P("tp"),
        P("tp"),
        P("tp", None),
        P(),
    )
    out_specs = P(("seq", "tp"), None)
    return jax.shard_map(body, mesh=mesh, in_specs=in_specs, out_specs=out_specs, check_vma=False)
```

profile of v0, /device:TPU:0, one launch (start us, length us, event | category | flops | bytes accessed | tf_op | source)
XLA Modules:
  0.0 372.5 jit_solution(9451892559120451516)
XLA Ops:
  6.6 1.7 fusion.20
  8.3 2.5 fusion.22
  11.6 1.2 reduce-window.16
  14.8 4.9 %copy.92 = bf16[512,8,2,256]{3,1,2,0:T(8,128)(2,1)} copy(bf16[512,8,2,256]{3,2,1,0:T(2,128)(2,1)} %bitcast.91) | data formatting | bytes 8388608
  21.1 74.7 %all-gather.4.cloned.1.call-done = bf16[1024,4096]{1,0:T(8,128)(2,1)} async-done(((bf16[128,4096]{1,0:T(8,128)(2,1)}), bf16[1024,4096]{1,0:T(8,128)(2,1)}) %all-gather.4.cloned.1.call-update) | async-done | bytes 8388624 | tf_op jit(solution)/shard_map/all_gather | solution.py:90
  95.8 5.7 %negate_multiply_fusion = (f32[1024,4]{0,1:T(4,128)S(1)}, f32[1024,4]{0,1:T(4,128)S(1)}) fusion(f32[4]{0:T(128)S(1)} %copy-done.15, f32[4]{0:T(128)S(1)} %copy-done.16, bf16[1024,4096]{1,0:T(8,128)(2,1)} %all-gather.4.cloned.1.call-done, bf16[4096,4]{0,1:T(4,128)(2,1)S(1)} %copy-done.13), kind=kOutput, calls=%fused_computation.96 | convolution fusion | flops 33591296 | bytes 8454176 | tf_op jit(solution)/shard_map/dot_general | solution.py:92
  101.5 4.8 %reduce-window.14 = f32[4,4,2,128]{3,2,1,0:T(2,128)S(1)} reduce-window(f32[4,4,2,128]{3,2,1,0:T(2,128)S(1)} %copy.83, f32[]{:T(128)} %constant.89.clone.1), window={size=1x1x1x128 pad=0_0x0_0x0_0x127_0}, to_apply=%region_1.2 | reduce-window | flops 520192 | bytes 32772 | tf_op jit(solution)/shard_map/reduce-window
  107.2 6.7 %fusion.38 = f32[1024,128]{0,1:T(8,128)S(1)} fusion(bf16[1024,4096]{1,0:T(8,128)(2,1)} %all-gather.4.cloned.1.call-done, bf16[4096,128]{1,0:T(8,128)(2,1)} %collective-permute-done.1, bf16[4096,128]{1,0:T(8,128)(2,1)S(1)} %copy-done.7, pred[]{:T(512)S(6)} %eq.59), kind=kOutput, calls=%fused_computation.58 | convolution fusion | flops 1074266112 | bytes 11010049 | tf_op jit(solution)/shard_map/dot_general | solution.py:92
  113.8 2.9 fusion.40
  116.8 6.5 %fusion.78 = f32[1024,512]{0,1:T(8,128)S(1)} fusion(bf16[1024,4096]{1,0:T(8,128)(2,1)S(1)} %copy-done.1, bf16[4096,512]{1,0:T(8,128)(2,1)} %bitcast.92), kind=kOutput, calls=%fused_computation.123 | convolution fusion | flops 4294967296 | bytes 14680064 | tf_op jit(solution)/shard_map/dot_general | solution.py:92
  123.4 3.6 collective-permute-start.2
  127.4 5.9 %collective-permute-done.2 = f32[3,512]{0,1:T(8,128)S(1)} collective-permute-done((f32[3,512]{0,1:T(8,128)S(1)}, f32[3,512]{0,1:T(8,128)S(1)}, u32[]{:S(2)}, u32[]{:S(2)}) %collective-permute-start.2) | collective-permute-done | bytes 6176 | tf_op jit(solution)/shard_map/ppermute | solution.py:24
  133.3 2.4 divide_multiply_fusion
  137.4 2.7 reshape.145
  141.1 3.4 fusion.36
  144.5 6.9 %while.31 = (s32[]{:T(128)}, f32[4,64,128]{2,1,0:T(8,128)S(1)}, f32[4]{0:T(128)S(1)}, f32[4,4,64,128]{3,2,1,0:T(8,128)}, f32[4,4]{1,0:T(4,128)S(1)}, /*index=5*/...) while((s32[]{:T(128)}, f32[4,64,128]{2,1,0:T(8,128)S(1)}, f32[4]{0:T(128)S(1)}, ...), condition=%wide.region_7.8_spmd.clone, body=%wide.region_6.7_spmd.clone.sunk | while | flops 131083 | bytes 655617 | solution.py:145
  152.7 10.8 %all-reduce.1 = f32[16]{0:T(128)S(1)} all-reduce(f32[16]{0:T(128)S(1)} %dynamic-update-slice), channel_id=2, replica_groups=mesh['seq'=4,'tp'=8] {'seq'}, use_global_device_ids=true, to_apply=%add.1 | all-reduce | flops 16 | bytes 128
  163.6 10.2 %all-gather.1 = f32[16,64,128]{2,1,0:T(8,128)} all-gather(f32[4,64,128]{2,1,0:T(8,128)S(1)} %get-tuple-element.142), channel_id=3, replica_groups=mesh['seq'=4,'tp'=8] {'seq'}, dimensions={0}, use_global_device_ids=true | all-gather | bytes 655360 | tf_op jit(solution)/shard_map/all_gather | solution.py:29
  173.8 3.1 while.32
  178.2 5.2 %fusion.33 = f32[4,256,4,64]{1,3,2,0:T(8,128)S(1)} fusion(f32[4,4,256]{2,1,0:T(4,128)S(1)} %copy.69, f32[4,256,256]{2,1,0:T(8,128)S(1)} %fusion.47, f32[4,4,256]{2,1,0:T(4,128)S(1)} %reduce_window_sum.41, pred[4,256,256]{2,1,0:T(8,128)(4,1)S(1)} %copy-done.11, f32[4,256,4,64]{1,0,3,2:T(4,128)S(1)} %copy-done.8), kind=kOutput, calls=%fused_computation.51 | convolution fusion | flops 810549248 | bytes 3440640 | tf_op jit(solution)/shard_map/chij,cjhp->cihp/dot_general | solution.py:128
  187.3 1.2 collective-permute-done.3
  188.4 8.2 %fusion.46 = f32[1024,4096]{1,0:T(8,128)} fusion(bf16[256,4096]{1,0:T(8,128)(2,1)S(1)} %copy-done, f32[1024,256]{0,1:T(8,128)S(1)} %get-tuple-element.213, f32[256]{0:T(256)S(1)} %copy-done.14, f32[1024]{0:T(1024)S(1)} %add_rsqrt_fusion), kind=kOutput, calls=%fused_computation.67 | convolution fusion | flops 2148270080 | bytes 19928064 | tf_op jit(solution)/shard_map/dot_general | solution.py:162
  196.7 166.2 %reduce-scatter.2.cloned.1.call-done = f32[128,4096]{1,0:T(8,128)} async-done(((f32[1024,4096]{1,0:T(8,128)}), f32[128,4096]{1,0:T(8,128)}) %reduce-scatter.2.cloned.1.call-update) | async-done | bytes 2097168 | tf_op jit(solution)/shard_map/reduce_scatter | solution.py:163
  362.8 2.8 fusion.23
  (135 shorter events, 23.7 us)
Async XLA Ops:
  6.5 181.9 %copy-start = (bf16[256,4096]{1,0:T(8,128)(2,1)S(1)}, bf16[256,4096]{1,0:T(8,128)(2,1)}, u32[]{:S(2)}) copy-start(bf16[256,4096]{1,0:T(8,128)(2,1)} %param.28) | copy-start | bytes 6291460
  6.5 4.3 %copy-start.18 = (bf16[4,128]{1,0:T(4,128)(2,1)S(1)}, bf16[4,128]{1,0:T(4,128)(2,1)}, u32[]{:S(2)}) copy-start(bf16[4,128]{1,0:T(4,128)(2,1)} %param.25) | copy-start | bytes 3076
  6.5 4.9 %copy-start.7 = (bf16[4096,128]{1,0:T(8,128)(2,1)S(1)}, bf16[4096,128]{1,0:T(8,128)(2,1)}, u32[]{:S(2)}) copy-start(bf16[4096,128]{1,0:T(8,128)(2,1)} %param.20) | copy-start | bytes 3145732
  6.5 5.0 %copy-start.12 = (s32[4096]{0:T(1024)S(1)}, s32[4096]{0:T(1024)}, u32[]{:S(2)}) copy-start(s32[4096]{0:T(1024)} %param.29) | copy-start | bytes 49156
  6.5 89.2 %all-gather.4.cloned.1.call-start = ((), (), s32[]{:S(2)}) async-start(), calls=%async_computation.1 | async-start | bytes 9437184 | tf_op jit(solution)/shard_map/all_gather | solution.py:90
  8.3 6.3 %copy-start.19 = (f32[4]{0:T(128)S(1)}, f32[4]{0:T(128)}, u32[]{:S(2)}) copy-start(f32[4]{0:T(128)} %param.26) | copy-start | bytes 52
  10.8 352.0 %reduce-scatter.2.cloned.1.call-start = ((), (), s32[]{:S(2)}) async-start(), calls=%async_computation.2 | async-start | bytes 18874368 | tf_op jit(solution)/shard_map/reduce_scatter | solution.py:163
  10.9 10.1 %collective-permute-start = (bf16[4,128]{1,0:T(4,128)(2,1)S(1)}, bf16[4,128]{1,0:T(4,128)(2,1)S(1)}, u32[]{:S(2)}, u32[]{:S(2)}) collective-permute-start(bf16[4,128]{1,0:T(4,128)(2,1)S(1)} %copy-done.18), channel_id=1, source_target_pairs={{0,1},{1,0},{2,3},{3,2},{4,5},{5,4},{6,7},{7,6},{8,9},{9,8},{10,11... | collective-permute-start | bytes 3080 | tf_op jit(solution)/shard_map/ppermute | solution.py:18
  11.4 95.7 %collective-permute-start.1 = (bf16[4096,128]{1,0:T(8,128)(2,1)S(1)}, bf16[4096,128]{1,0:T(8,128)(2,1)}, u32[]{:S(2)}, u32[]{:S(2)}) collective-permute-start(bf16[4096,128]{1,0:T(8,128)(2,1)S(1)} %copy-done.7), channel_id=1, source_target_pairs={{0,1},{1,0},{2,3},{3,2},{4,5},{5,4},{6,7},{7,6},{8,9},{9,8},{10,11... | collective-permute-start | bytes 3145736 | tf_op jit(solution)/shard_map/ppermute | solution.py:18
  14.8 5.0 %copy-start.20 = (u32[32]{0:T(128)S(1)}, u32[32]{0:T(128)}, u32[]{:S(2)}) copy-start(u32[32]{0:T(128)} %constant.107) | copy-start | bytes 388
  14.8 6.3 %copy-start.17 = (bf16[4,256]{1,0:T(4,128)(2,1)S(1)}, bf16[4,256]{1,0:T(4,128)(2,1)}, u32[]{:S(2)}) copy-start(bf16[4,256]{1,0:T(4,128)(2,1)} %param.24) | copy-start | bytes 6148
  14.8 81.0 %copy-start.13 = (bf16[4096,4]{0,1:T(4,128)(2,1)S(1)}, bf16[4096,4]{0,1:T(4,128)(2,1)}, u32[]{:S(2)}) copy-start(bf16[4096,4]{0,1:T(4,128)(2,1)} %param.21) | copy-start | bytes 98308
  14.8 81.0 %copy-start.15 = (f32[4]{0:T(128)S(1)}, f32[4]{0:T(128)}, u32[]{:S(2)}) copy-start(f32[4]{0:T(128)} %param.23) | copy-start | bytes 52
  14.8 81.0 %copy-start.16 = (f32[4]{0:T(128)S(1)}, f32[4]{0:T(128)}, u32[]{:S(2)}) copy-start(f32[4]{0:T(128)} %param.22) | copy-start | bytes 52
  107.1 6.7 %copy-start.1 = (bf16[1024,4096]{1,0:T(8,128)(2,1)S(1)}, bf16[1024,4096]{1,0:T(8,128)(2,1)}, u32[]{:S(2)}) copy-start(bf16[1024,4096]{1,0:T(8,128)(2,1)} %all-gather.4.cloned.1.call-done) | copy-start | bytes 25165828
  123.3 4.1 %copy-start.4 = (f32[1024,512]{0,1:T(8,128)}, f32[1024,512]{0,1:T(8,128)S(1)}, u32[]{:S(2)}) copy-start(f32[1024,512]{0,1:T(8,128)S(1)} %fusion.78) | copy-start | bytes 6291460
  123.4 9.8 %collective-permute-start.2 = (f32[3,512]{0,1:T(8,128)S(1)}, f32[3,512]{0,1:T(8,128)S(1)}, u32[]{:S(2)}, u32[]{:S(2)}) collective-permute-start(f32[3,512]{0,1:T(8,128)S(1)} %pad_maximum_fusion.3), channel_id=1, source_target_pairs={{0,8},{8,16},{16,24},{1,9},{9,17},{17,25},{2,10},{10,18},{18,26},{... | collective-permute-start | bytes 18440 | tf_op jit(solution)/shard_map/ppermute | solution.py:24
  135.6 1.6 copy-start.2
  178.2 5.2 %copy-start.9 = (f32[4,256,128]{1,0,2:T(4,128)S(1)}, f32[4,256,128]{1,0,2:T(4,128)}, u32[]{:S(2)}) copy-start(f32[4,256,128]{1,0,2:T(4,128)} %reshape.149) | copy-start | bytes 1572868
  178.2 5.2 %copy-start.10 = (f32[4,4,64,128]{3,2,1,0:T(8,128)S(1)}, f32[4,4,64,128]{3,2,1,0:T(8,128)}, u32[]{:S(2)}) copy-start(f32[4,4,64,128]{3,2,1,0:T(8,128)} %get-tuple-element.139) | copy-start | bytes 1572868
  184.6 2.2 copy-start.5
  186.8 1.7 copy-start.14
  187.2 1.2 collective-permute-start.3
  196.7 166.2 %copy-start.6 = (bf16[128,4096]{1,0:T(8,128)(2,1)S(1)}, bf16[128,4096]{1,0:T(8,128)(2,1)}, u32[]{:S(2)}) copy-start(bf16[128,4096]{1,0:T(8,128)(2,1)} %param.17) | copy-start | bytes 3145732
  (3 other events, 4.1 us)
Sparse Core Ops, SparseCore 0:
  10.9 84.7 all-gather.3
  196.8 165.9 reduce-scatter.1
where the time goes:
time: 373 us; the launch traced here: 372 us
  waiting for transfers between devices  248 us (66%)
  matrix products  40.7 us (11%)
  other arithmetic  27.4 us (7%)
  blocking collectives  21.1 us (6%)
  local copies, waits for them, and re-layouts  16.4 us (4%)
  between operations  14.5 us (4%)
  starting transfers between devices  4.37 us (1%)
    reduce_scatter x1, waiting for transfers between devices, body(): mine = lax.psum_scatter(partial_out, 'tp', scatter_dimension=0, tiled=True)  166 us
    all_gather x1, waiting for transfers between devices, body(): piece = lax.all_gather(normed, 'tp', axis=0, tiled=True)  74.7 us
    dot_general x4, matrix products, body(): jnp.dot(piece, matrix, preferred_element_type=jnp.float32)  21.8 us
    unnamed x1, blocking collectives  10.8 us
    all_gather x1, blocking collectives, entering_2(): pieces = jax.tree.map(lambda part: lax.all_gather(part, axis), value)  10.2 us
    unnamed x49, local copies, waits for them, and re-layouts  8.25 us
    dot_general x1, matrix products, body(): jnp.dot(mixed, output_weight, preferred_element_type=jnp.float32)  8.21 us
  transfers between devices with their start and end apart: 6, of which 4 were waited for; matrix products, arithmetic and copies ran while one was open for 5% of the time, Pallas kernels for 0%

commit v1 on v0

--- a/solution.py
+++ b/solution.py
@@ -6,6 +6,17 @@
 STRETCH = 256
 EPS = 1e-05
 HIGH = lax.Precision.HIGHEST
+
+
+def pass_along(value, axis, dim):
+    size = lax.axis_size(axis)
+    hops = [(i, (i + 1) % size) for i in range(size)]
+    pieces = [value]
+    for hop in range(1, size):
+        pieces = [lax.ppermute(pieces[0], axis, hops), *pieces]
+    full = jnp.concatenate(pieces, axis=dim)
+    shift = (lax.axis_index(axis) + 1) * pieces[-1].shape[dim]
+    return jnp.roll(full, shift, axis=dim)
 
 
 def swapped(block, axis, stride):
@@ -87,7 +98,7 @@
         axis=1,
     )
     matrices = (inner_weight.reshape(width, 2 * inner_dev),) + group_cols + (step_weight,)
-    piece = lax.all_gather(normed, "tp", axis=0, tiled=True)
+    piece = pass_along(normed, "tp", 0)
     projected = jnp.concatenate(
         [jnp.dot(piece, matrix, preferred_element_type=jnp.float32) for matrix in matrices], axis=1
     )

time: 373 us -> 435 us (1.17)
  local copies, waits for them, and re-layouts: 16.4 us -> 47.9 us
  waiting for transfers between devices: 248 us -> 269 us
  matrix products: 40.7 us -> 45.7 us
    ppermute x0 -> x7, waiting for transfers between devices: none -> 101 us  [pass_along(): pieces = [lax.ppermute(pieces[0], axis, hops), *pieces]]
    all_gather x1 -> x0, waiting for transfers between devices: 74.7 us -> none  [body(): piece = lax.all_gather(normed, 'tp', axis=0, tiled=True)]
    unnamed x49 -> x85, local copies, waits for them, and re-layouts: 8.25 us -> 25.8 us
    dynamic_update_slice x4, local copies, waits for them, and re-layouts: 0.16 us -> 4.97 us  [body(): lax.scan(carry_blocks, (empty_state, unit_keep), (block_keep, block_state))]
  transfers between devices with their start and end apart: 6 -> 12, of which waited for: 4 -> 10; matrix products, arithmetic and copies ran while one was open for 5% -> 9% of each run, Pallas kernels for 0% -> 0%
where the time goes in v1:
time: 435 us; the launch traced here: 434 us
  waiting for transfers between devices  269 us (62%)
  local copies, waits for them, and re-layouts  47.9 us (11%)
  matrix products  45.7 us (11%)
  other arithmetic  29.2 us (7%)
  blocking collectives  22.2 us (5%)
  between operations  14.8 us (3%)
  starting transfers between devices  5.19 us (1%)
    reduce_scatter x1, waiting for transfers between devices, body(): mine = lax.psum_scatter(partial_out, 'tp', scatter_dimension=0, tiled=True)  165 us
    ppermute x7, waiting for transfers between devices, pass_along(): pieces = [lax.ppermute(pieces[0], axis, hops), *pieces]  101 us
    unnamed x85, local copies, waits for them, and re-layouts  25.8 us
    dot_general x4, matrix products, body(): jnp.dot(piece, matrix, preferred_element_type=jnp.float32)  24.2 us
    all_gather x1, blocking collectives, entering_2(): pieces = jax.tree.map(lambda part: lax.all_gather(part, axis), value)  12.6 us
    unnamed x1, blocking collectives  9.62 us
  transfers between devices with their start and end apart: 12, of which 10 were waited for; matrix products, arithmetic and copies ran while one was open for 9% of the time, Pallas kernels for 0%

profile of v1, /device:TPU:0, one launch (start us, length us, event | category | flops | bytes accessed | tf_op | source)
XLA Modules:
  0.0 434.2 jit_solution(1382030679393940975)
XLA Ops:
  10.3 16.5 %collective-permute-done.1 = bf16[128,4096]{1,0:T(8,128)(2,1)S(1)} collective-permute-done((bf16[128,4096]{1,0:T(8,128)(2,1)S(1)}, bf16[128,4096]{1,0:T(8,128)(2,1)S(1)}, u32[]{:S(2)}, u32[]{:S(2)}) %collective-permute-start.1) | collective-permute-done | bytes 1048608 | tf_op jit(solution)/shard_map/ppermute | solution.py:16
  26.8 16.0 %collective-permute-done.2 = bf16[128,4096]{1,0:T(8,128)(2,1)S(1)} collective-permute-done((bf16[128,4096]{1,0:T(8,128)(2,1)S(1)}, bf16[128,4096]{1,0:T(8,128)(2,1)S(1)}, u32[]{:S(2)}, u32[]{:S(2)}) %collective-permute-start.2) | collective-permute-done | bytes 1048608 | tf_op jit(solution)/shard_map/ppermute | solution.py:16
  43.8 16.0 %collective-permute-done.3 = bf16[128,4096]{1,0:T(8,128)(2,1)S(1)} collective-permute-done((bf16[128,4096]{1,0:T(8,128)(2,1)S(1)}, bf16[128,4096]{1,0:T(8,128)(2,1)S(1)}, u32[]{:S(2)}, u32[]{:S(2)}) %collective-permute-start.3) | collective-permute-done | bytes 1048608 | tf_op jit(solution)/shard_map/ppermute | solution.py:16
  60.8 16.0 %collective-permute-done.4 = bf16[128,4096]{1,0:T(8,128)(2,1)S(1)} collective-permute-done((bf16[128,4096]{1,0:T(8,128)(2,1)S(1)}, bf16[128,4096]{1,0:T(8,128)(2,1)S(1)}, u32[]{:S(2)}, u32[]{:S(2)}) %collective-permute-start.4) | collective-permute-done | bytes 1048608 | tf_op jit(solution)/shard_map/ppermute | solution.py:16
  77.8 16.1 %collective-permute-done.5 = bf16[128,4096]{1,0:T(8,128)(2,1)} collective-permute-done((bf16[128,4096]{1,0:T(8,128)(2,1)S(1)}, bf16[128,4096]{1,0:T(8,128)(2,1)}, u32[]{:S(2)}, u32[]{:S(2)}) %collective-permute-start.5) | collective-permute-done | bytes 1048608 | tf_op jit(solution)/shard_map/ppermute | solution.py:16
  97.2 13.0 %collective-permute-done.6 = bf16[128,4096]{1,0:T(8,128)(2,1)} collective-permute-done((bf16[128,4096]{1,0:T(8,128)(2,1)}, bf16[128,4096]{1,0:T(8,128)(2,1)}, u32[]{:S(2)}, u32[]{:S(2)}) %collective-permute-start.6) | collective-permute-done | bytes 1048608 | tf_op jit(solution)/shard_map/ppermute | solution.py:16
  112.2 4.9 %copy.92 = bf16[512,8,2,256]{3,1,2,0:T(8,128)(2,1)} copy(bf16[512,8,2,256]{3,2,1,0:T(2,128)(2,1)} %bitcast.87) | data formatting | bytes 8388608
  119.2 7.4 %collective-permute-done.7 = bf16[128,4096]{1,0:T(8,128)(2,1)} collective-permute-done((bf16[128,4096]{1,0:T(8,128)(2,1)}, bf16[128,4096]{1,0:T(8,128)(2,1)}, u32[]{:S(2)}, u32[]{:S(2)}) %collective-permute-start.7) | collective-permute-done | bytes 1048608 | tf_op jit(solution)/shard_map/ppermute | solution.py:16
  137.3 5.7 %copy-done.6 = bf16[2048,4096]{1,0:T(8,128)(2,1)} copy-done((bf16[2048,4096]{1,0:T(8,128)(2,1)}, bf16[2048,4096]{1,0:T(8,128)(2,1)S(1)}, u32[]{:S(2)}) %copy-start.6) | copy-done | bytes 16777240
  145.4 4.8 %reduce-window.14 = f32[4,4,2,128]{3,2,1,0:T(2,128)S(1)} reduce-window(f32[4,4,2,128]{3,2,1,0:T(2,128)S(1)} %copy.83, f32[]{:T(128)} %constant.109.clone.1), window={size=1x1x1x128 pad=0_0x0_0x0_0x127_0}, to_apply=%region_1.2 | reduce-window | flops 520192 | bytes 32772 | tf_op jit(solution)/shard_map/reduce-window
  151.0 8.3 %fusion.10 = f32[1024,512]{0,1:T(8,128)S(1)} fusion(bf16[4096,512]{1,0:T(8,128)(2,1)} %bitcast.88, bf16[2048,4096]{1,0:T(8,128)(2,1)} %copy-done.6, s32[]{:T(128)S(6)} %select_n.93), kind=kOutput, calls=%fused_computation.16 | convolution fusion | flops 4294967296 | bytes 14680068 | tf_op jit(solution)/shard_map/dot_general | solution.py:103
  159.4 7.3 %fusion.6 = f32[1024,128]{0,1:T(8,128)S(1)} fusion(bf16[2048,4096]{1,0:T(8,128)(2,1)} %copy-done.6, s32[]{:T(128)S(6)} %select_n.93, bf16[4096,128]{1,0:T(8,128)(2,1)} %collective-permute-done.8, bf16[4096,128]{1,0:T(8,128)(2,1)S(1)} %copy-done.29, pred[]{:T(512)S(6)} %eq.62), kind=kOutput, calls=%fused_computation.12 | convolution fusion | flops 1074266112 | bytes 11010053 | tf_op jit(solution)/shard_map/dot_general | solution.py:103
  166.7 6.3 %fusion.8 = f32[1024,128]{0,1:T(8,128)S(1)} fusion(bf16[2048,4096]{1,0:T(8,128)(2,1)} %copy-done.6, s32[]{:T(128)S(6)} %select_n.93, bf16[4096,128]{1,0:T(8,128)(2,1)S(1)} %copy-done.29, bf16[4096,128]{1,0:T(8,128)(2,1)} %collective-permute-done.8, pred[]{:T(512)S(6)} %eq.62), kind=kOutput, calls=%fused_computation.14 | convolution fusion | flops 1074266112 | bytes 11010053 | tf_op jit(solution)/shard_map/dot_general | solution.py:103
  173.1 4.1 collective-permute-start.9
  186.0 2.7 reshape.145
  190.7 3.4 fusion.47
  194.1 11.6 %while.31 = (s32[]{:T(128)}, f32[4,64,128]{2,1,0:T(8,128)S(1)}, f32[4]{0:T(128)S(1)}, f32[4,4,64,128]{3,2,1,0:T(8,128)}, f32[4,4]{1,0:T(4,128)}, /*index=5*/f32[...) while((s32[]{:T(128)}, f32[4,64,128]{2,1,0:T(8,128)S(1)}, f32[4]{0:T(128)S(1)}, ...), condition=%wide.region_7.8_spmd.clone, body=%wide.region_6.7_spmd.clone.sunk | while | flops 131083 | bytes 656117 | solution.py:156
  206.4 12.6 %all-gather.1 = f32[16,64,128]{2,1,0:T(8,128)} all-gather(f32[4,64,128]{2,1,0:T(8,128)S(1)} %get-tuple-element.142), channel_id=3, replica_groups=mesh['seq'=4,'tp'=8] {'seq'}, dimensions={0}, use_global_device_ids=true | all-gather | bytes 655360 | tf_op jit(solution)/shard_map/all_gather | solution.py:40
  219.0 9.6 %all-reduce.1 = f32[16]{0:T(128)} all-reduce(f32[16]{0:T(128)} %copy-done.31), channel_id=2, replica_groups=mesh['seq'=4,'tp'=8] {'seq'}, use_global_device_ids=true, to_apply=%add.1 | all-reduce | flops 16 | bytes 128
  229.9 6.8 %while.32 = (s32[]{:T(128)}, f32[4,64,128]{2,1,0:T(8,128)S(1)}, s32[]{:T(128)}, f32[4,4]{1,0:T(4,128)}, f32[4,4,64,128]{3,2,1,0:T(8,128)}, /*index=5*/s32[]{:T(128)}, s32[]{:T(128)}) while((s32[]{:T(128)}, f32[4,64,128]{2,1,0:T(8,128)S(1)}, s32[]{:T(128)}, f32[4,4]{1,0:T(4,128)}, f32[4,4,64,128]{3,2,1,0:T(8,128)}, ...), condition=%wide.region_9.10_spmd.clone, body=%wide.region_8.9_spmd.clone.sunk | while | flops 131076 | bytes 393369 | solution.py:49
  241.0 6.6 %fusion.41 = f32[4,256,4,64]{1,3,2,0:T(8,128)S(1)} fusion(f32[4,4,256]{2,1,0:T(4,128)} %copy.69, f32[4,256,256]{2,1,0:T(8,128)S(1)} %fusion.56, f32[4,4,256]{2,1,0:T(4,128)S(1)} %reduce_window_sum.41, pred[4,256,256]{2,1,0:T(8,128)(4,1)S(1)} %copy-done.17, f32[4,256,4,64]{1,0,3,2:T(4,128)} %reshape.145), kind=kOutput, calls=%fused_computation.59 | convolution fusion | flops 810549248 | bytes 3440640 | tf_op jit(solution)/shard_map/chij,cjhp->cihp/dot_general | solution.py:139
  251.5 8.2 %fusion.55 = f32[1024,4096]{1,0:T(8,128)} fusion(bf16[256,4096]{1,0:T(8,128)(2,1)S(1)} %copy-done, f32[1024,256]{0,1:T(8,128)S(1)} %get-tuple-element.213, f32[256]{0:T(256)S(1)} %copy-done.21, f32[1024]{0:T(1024)S(1)} %add_rsqrt_fusion), kind=kOutput, calls=%fused_computation.73 | convolution fusion | flops 2148270080 | bytes 19928064 | tf_op jit(solution)/shard_map/dot_general | solution.py:173
  259.8 164.8 %reduce-scatter.2.cloned.1.call-done = f32[128,4096]{1,0:T(8,128)} async-done(((f32[1024,4096]{1,0:T(8,128)}), f32[128,4096]{1,0:T(8,128)}) %reduce-scatter.2.cloned.1.call-update) | async-done | bytes 2097168 | tf_op jit(solution)/shard_map/reduce_scatter | solution.py:174
  424.5 2.8 fusion.31
  (184 shorter events, 66.1 us)
Async XLA Ops:
  6.5 245.0 %copy-start = (bf16[256,4096]{1,0:T(8,128)(2,1)S(1)}, bf16[256,4096]{1,0:T(8,128)(2,1)}, u32[]{:S(2)}) copy-start(bf16[256,4096]{1,0:T(8,128)(2,1)} %param.28) | copy-start | bytes 6291460
  6.5 418.0 %reduce-scatter.2.cloned.1.call-start = ((), (), s32[]{:S(2)}) async-start(), calls=%async_computation.1 | async-start | bytes 18874368 | tf_op jit(solution)/shard_map/reduce_scatter | solution.py:174
  9.8 17.0 %collective-permute-start.1 = (bf16[128,4096]{1,0:T(8,128)(2,1)S(1)}, bf16[128,4096]{1,0:T(8,128)(2,1)S(1)}, u32[]{:S(2)}, u32[]{:S(2)}) collective-permute-start(bf16[128,4096]{1,0:T(8,128)(2,1)S(1)} %fusion.30), channel_id=1, source_target_pairs={{0,1},{1,2},{2,3},{3,4},{4,5},{5,6},{6,7},{7,0},{8,9},{9,10},{10,1... | collective-permute-start | bytes 3145736 | tf_op jit(solution)/shard_map/ppermute | solution.py:16
  26.8 83.6 %copy-start.7 = (bf16[128,4096]{1,0:T(8,128)(2,1)}, bf16[128,4096]{1,0:T(8,128)(2,1)S(1)}, u32[]{:S(2)}) copy-start(bf16[128,4096]{1,0:T(8,128)(2,1)S(1)} %collective-permute-done.1) | copy-start | bytes 3145732
  26.8 16.0 %collective-permute-start.2 = (bf16[128,4096]{1,0:T(8,128)(2,1)S(1)}, bf16[128,4096]{1,0:T(8,128)(2,1)S(1)}, u32[]{:S(2)}, u32[]{:S(2)}) collective-permute-start(bf16[128,4096]{1,0:T(8,128)(2,1)S(1)} %collective-permute-done.1), channel_id=1, source_target_pairs={{0,1},{1,2},{2,3},{3,4},{4,5},{5,6},{6,7},{7,0},{8,9},{9,10},{10,1... | collective-permute-start | bytes 3145736 | tf_op jit(solution)/shard_map/ppermute | solution.py:16
  43.8 16.0 %collective-permute-start.3 = (bf16[128,4096]{1,0:T(8,128)(2,1)S(1)}, bf16[128,4096]{1,0:T(8,128)(2,1)S(1)}, u32[]{:S(2)}, u32[]{:S(2)}) collective-permute-start(bf16[128,4096]{1,0:T(8,128)(2,1)S(1)} %collective-permute-done.2), channel_id=1, source_target_pairs={{0,1},{1,2},{2,3},{3,4},{4,5},{5,6},{6,7},{7,0},{8,9},{9,10},{10,1... | collective-permute-start | bytes 3145736 | tf_op jit(solution)/shard_map/ppermute | solution.py:16
  60.8 16.0 %collective-permute-start.4 = (bf16[128,4096]{1,0:T(8,128)(2,1)S(1)}, bf16[128,4096]{1,0:T(8,128)(2,1)S(1)}, u32[]{:S(2)}, u32[]{:S(2)}) collective-permute-start(bf16[128,4096]{1,0:T(8,128)(2,1)S(1)} %collective-permute-done.3), channel_id=1, source_target_pairs={{0,1},{1,2},{2,3},{3,4},{4,5},{5,6},{6,7},{7,0},{8,9},{9,10},{10,1... | collective-permute-start | bytes 3145736 | tf_op jit(solution)/shard_map/ppermute | solution.py:16
  77.8 16.1 %collective-permute-start.5 = (bf16[128,4096]{1,0:T(8,128)(2,1)S(1)}, bf16[128,4096]{1,0:T(8,128)(2,1)}, u32[]{:S(2)}, u32[]{:S(2)}) collective-permute-start(bf16[128,4096]{1,0:T(8,128)(2,1)S(1)} %collective-permute-done.4), channel_id=1, source_target_pairs={{0,1},{1,2},{2,3},{3,4},{4,5},{5,6},{6,7},{7,0},{8,9},{9,10},{10,1... | collective-permute-start | bytes 3145736 | tf_op jit(solution)/shard_map/ppermute | solution.py:16
  93.9 16.3 %collective-permute-start.6 = (bf16[128,4096]{1,0:T(8,128)(2,1)}, bf16[128,4096]{1,0:T(8,128)(2,1)}, u32[]{:S(2)}, u32[]{:S(2)}) collective-permute-start(bf16[128,4096]{1,0:T(8,128)(2,1)} %collective-permute-done.5), channel_id=1, source_target_pairs={{0,1},{1,2},{2,3},{3,4},{4,5},{5,6},{6,7},{7,0},{8,9},{9,10},{10,1... | collective-permute-start | bytes 3145736 | tf_op jit(solution)/shard_map/ppermute | solution.py:16
  93.9 65.4 %collective-permute-start.8 = (bf16[4096,128]{1,0:T(8,128)(2,1)}, bf16[4096,128]{1,0:T(8,128)(2,1)}, u32[]{:S(2)}, u32[]{:S(2)}) collective-permute-start(bf16[4096,128]{1,0:T(8,128)(2,1)} %param.20), channel_id=1, source_target_pairs={{0,1},{1,0},{2,3},{3,2},{4,5},{5,4},{6,7},{7,6},{8,9},{9,8},{10,11... | collective-permute-start | bytes 3145736 | tf_op jit(solution)/shard_map/ppermute | solution.py:29
  93.9 25.1 %collective-permute-start = (bf16[4,128]{1,0:T(4,128)(2,1)}, bf16[4,128]{1,0:T(4,128)(2,1)S(1)}, u32[]{:S(2)}, u32[]{:S(2)}) collective-permute-start(bf16[4,128]{1,0:T(4,128)(2,1)} %param.25), channel_id=1, source_target_pairs={{0,1},{1,0},{2,3},{3,2},{4,5},{5,4},{6,7},{7,6},{8,9},{9,8},{10,11... | collective-permute-start | bytes 3080 | tf_op jit(solution)/shard_map/ppermute | solution.py:29
  110.3 16.3 %collective-permute-start.7 = (bf16[128,4096]{1,0:T(8,128)(2,1)}, bf16[128,4096]{1,0:T(8,128)(2,1)}, u32[]{:S(2)}, u32[]{:S(2)}) collective-permute-start(bf16[128,4096]{1,0:T(8,128)(2,1)} %collective-permute-done.6), channel_id=1, source_target_pairs={{0,1},{1,2},{2,3},{3,4},{4,5},{5,6},{6,7},{7,0},{8,9},{9,10},{10,1... | collective-permute-start | bytes 3145736 | tf_op jit(solution)/shard_map/ppermute | solution.py:16
  112.2 6.9 %copy-start.27 = (bf16[4,128]{1,0:T(4,128)(2,1)S(1)}, bf16[4,128]{1,0:T(4,128)(2,1)}, u32[]{:S(2)}) copy-start(bf16[4,128]{1,0:T(4,128)(2,1)} %param.25) | copy-start | bytes 3076
  112.2 6.9 %copy-start.25 = (bf16[4,256]{1,0:T(4,128)(2,1)S(1)}, bf16[4,256]{1,0:T(4,128)(2,1)}, u32[]{:S(2)}) copy-start(bf16[4,256]{1,0:T(4,128)(2,1)} %param.24) | copy-start | bytes 6148
  119.2 13.0 %copy-start.12 = (bf16[128,4096]{1,0:T(8,128)(2,1)S(1)}, bf16[128,4096]{1,0:T(8,128)(2,1)}, u32[]{:S(2)}) copy-start(bf16[128,4096]{1,0:T(8,128)(2,1)} %copy-done.11) | copy-start | bytes 3145732
  151.0 8.4 %copy-start.29 = (bf16[4096,128]{1,0:T(8,128)(2,1)S(1)}, bf16[4096,128]{1,0:T(8,128)(2,1)}, u32[]{:S(2)}) copy-start(bf16[4096,128]{1,0:T(8,128)(2,1)} %param.20) | copy-start | bytes 3145732
  159.4 18.6 %copy-start.4 = (f32[1024,512]{0,1:T(8,128)}, f32[1024,512]{0,1:T(8,128)S(1)}, u32[]{:S(2)}) copy-start(f32[1024,512]{0,1:T(8,128)S(1)} %fusion.10) | copy-start | bytes 6291460
  173.1 7.8 %collective-permute-start.9 = (f32[3,512]{0,1:T(8,128)S(1)}, f32[3,512]{0,1:T(8,128)S(1)}, u32[]{:S(2)}, u32[]{:S(2)}) collective-permute-start(f32[3,512]{0,1:T(8,128)S(1)} %pad_maximum_fusion.3), channel_id=1, source_target_pairs={{0,8},{8,16},{16,24},{1,9},{9,17},{17,25},{2,10},{10,18},{18,26},{... | collective-permute-start | bytes 18440 | tf_op jit(solution)/shard_map/ppermute | solution.py:35
  219.0 22.0 %copy-start.17 = (pred[4,256,256]{2,1,0:T(8,128)(4,1)S(1)}, pred[4,256,256]{2,1,0:T(8,128)(4,1)}, u32[]{:S(2)}) copy-start(pred[4,256,256]{2,1,0:T(8,128)(4,1)} %compare_and_fusion) | copy-start | bytes 786436
  241.0 6.7 %copy-start.15 = (f32[4,256,128]{1,0,2:T(4,128)S(1)}, f32[4,256,128]{1,0,2:T(4,128)}, u32[]{:S(2)}) copy-start(f32[4,256,128]{1,0,2:T(4,128)} %reshape.149) | copy-start | bytes 1572868
  241.0 6.7 %copy-start.16 = (f32[4,4,64,128]{3,2,1,0:T(8,128)S(1)}, f32[4,4,64,128]{3,2,1,0:T(8,128)}, u32[]{:S(2)}) copy-start(f32[4,4,64,128]{3,2,1,0:T(8,128)} %get-tuple-element.139) | copy-start | bytes 1572868
  241.0 6.7 %copy-start.19 = (f32[4,256,4]{1,2,0:T(4,128)S(1)}, f32[4,256,4]{1,2,0:T(4,128)}, u32[]{:S(2)}) copy-start(f32[4,256,4]{1,2,0:T(4,128)} %multiply_bitcast_fusion) | copy-start | bytes 49156
  241.0 6.7 %copy-start.26 = (f32[4,4]{1,0:T(4,128)S(1)}, f32[4,4]{1,0:T(4,128)}, u32[]{:S(2)}) copy-start(f32[4,4]{1,0:T(4,128)} %get-tuple-element.140) | copy-start | bytes 196
  250.3 1.2 collective-permute-start.10
  (20 other events, 64.4 us)
Sparse Core Ops, SparseCore 0:
  259.9 164.6 reduce-scatter.1
